TPU v7x, 32 devices: a whole 2x2x4 slice. The times are simulated.
32 devices in a mesh: grp: 4 (over y, core), ch: 8 (over z, x).
Axes of the slice: x: 2, y: 2, z: 4, core: 2. Of those that a mesh axis runs over, the one named last changes fastest.
Arguments:
- strain: bfloat16 [8, 1024, 4096], P('grp', 'ch'), may hold values from -6 to 6
- valid_mask: int32 [8, 1024], P('grp', 'ch'), may hold values 0 or 1
- pair_list: int32 [8, 6, 2], P('ch'), may hold values from 0 to 7, as said below
- owner_group: int32 [8, 6], P('ch'), may hold values from 0 to 3, as said below
Outputs:
- stacks: float32 [4, 8, 2, 128, 4096], P('grp', 'ch')
Inputs may be any that keep to these rules, and one draw needn't show every extreme that they name: `pair_list`: entries are channel block numbers; each ordered pair of blocks appears at most once over all columns. `owner_group`: in each column no group owns more than 2 entries, and some group owns exactly 2.
All inputs are finite; a program needn't handle non-finite values. No bound on the sum of `valid_mask` on one device may be relied on, other than what follows from the above.
Results may differ from a plain program's by a relative error of at most 0.0042.
Values may be sent and summed in bfloat16 or wider, within the bound.
A program may use at most 192 MiB of HBM per device.

v0:
```python
import math
import jax
import jax.numpy as jnp
from jax import lax
from jax.sharding import PartitionSpec as P

NFFT = 4096
NB = 1024
SUB = 64
BLK = 128
CAP = 2


def forward_table(length, bins):
    samples = jnp.arange(length, dtype=jnp.int32)
    frequency = jnp.arange(1, bins + 1, dtype=jnp.int32)
    angles = jnp.mod(samples[:, None] * frequency[None, :], length).astype(jnp.float32) * (
        2.0 * math.pi / length
    )
    hann_taper = 0.5 - 0.5 * jnp.cos(samples.astype(jnp.float32) * (2.0 * math.pi / length))
    return jnp.concatenate(
        [hann_taper[:, None] * jnp.cos(angles), -hann_taper[:, None] * jnp.sin(angles)], axis=1
    ).astype(jnp.bfloat16)


def inverse_table(length, bins):
    frequency = jnp.arange(1, bins + 1, dtype=jnp.int32)
    lag_index = jnp.arange(length, dtype=jnp.int32) - length // 2
    angles = jnp.mod(frequency[:, None] * lag_index[None, :], length).astype(jnp.float32) * (
        2.0 * math.pi / length
    )
    return jnp.concatenate([jnp.cos(angles), -jnp.sin(angles)], axis=0)


def whiten_rows(spectrum, valid_mask, bins, band):
    real_part = spectrum[..., :bins]
    imag_part = spectrum[..., bins:]
    power = real_part * real_part + imag_part * imag_part
    band_power = jnp.sum(power.reshape(power.shape[:-1] + (bins // band, band)), axis=-1) / band
    norm_full = jnp.repeat(jnp.sqrt(band_power + 1e-06), band, axis=-1)
    norm_both = jnp.concatenate([norm_full, norm_full], axis=-1)
    return (spectrum / norm_both * valid_mask[..., None].astype(jnp.float32)).astype(jnp.bfloat16)


def cross_block(rows, pair_entry, block, bins):
    first_rows = lax.dynamic_slice_in_dim(rows, pair_entry[0] * block, block, 1).astype(jnp.float32)
    second_rows = lax.dynamic_slice_in_dim(rows, pair_entry[1] * block, block, 1).astype(
        jnp.float32
    )
    first_real = first_rows[..., :bins]
    first_imag = first_rows[..., bins:]
    second_real = second_rows[..., :bins]
    second_imag = second_rows[..., bins:]
    cross_real = jnp.sum(first_real * second_real + first_imag * second_imag, axis=0)
    cross_imag = jnp.sum(first_real * second_imag - first_imag * second_real, axis=0)
    return jnp.concatenate([cross_real, cross_imag], axis=-1)


def local(strain, valid_mask, pair_list, owner_group):
    window_count = strain.shape[0]
    groups = lax.axis_size("grp")
    forward = forward_table(NFFT, NB)
    spectrum = jnp.dot(strain.reshape(-1, NFFT), forward, preferred_element_type=jnp.float32)
    spectrum = spectrum.reshape(strain.shape[0], strain.shape[1], 2 * NB)
    white = whiten_rows(spectrum, valid_mask, NB, SUB)
    gathered = lax.all_gather(white, "ch", axis=1, tiled=True)
    pair_codes = pair_list[0]
    partial_value = lax.map(
        lambda pair_entry: cross_block(gathered, pair_entry, BLK, NB), pair_codes
    )
    owners = owner_group[0]
    list_len = owners.shape[0]
    positions = jnp.arange(list_len, dtype=jnp.int32)
    earlier = positions[None, :] < positions[:, None]
    slot_rank = jnp.sum(((owners[:, None] == owners[None, :]) & earlier).astype(jnp.int32), axis=1)
    slot_ids = jnp.arange(CAP, dtype=jnp.int32)
    flat_partial = partial_value.reshape(list_len, -1)
    summed = lax.psum(flat_partial, "grp")
    my_group = lax.axis_index("grp")
    picking = ((owners[None, :] == my_group) & (slot_rank[None, :] == slot_ids[:, None])).astype(
        jnp.float32
    )
    total = jnp.dot(
        picking, summed, precision=lax.Precision.HIGHEST, preferred_element_type=jnp.float32
    )
    inverse = inverse_table(NFFT, NB)
    stacked = jnp.dot(
        total.reshape(-1, 2 * NB),
        inverse,
        precision=lax.Precision.HIGHEST,
        preferred_element_type=jnp.float32,
    )
    scale = 1.0 / math.sqrt(NB * window_count * groups)
    return (stacked * scale).reshape(1, 1, CAP, BLK, NFFT)


def solution(mesh):
    placed = (P("grp", "ch", None), P("grp", "ch"), P("ch", None, None), P("ch", None))
    return jax.shard_map(
        local,
        mesh=mesh,
        in_specs=placed,
        out_specs=P("grp", "ch", None, None, None),
        check_vma=False,
    )
```

profile of v0, /device:TPU:0, one launch (start us, length us, event | category | flops | bytes accessed | tf_op | source)
XLA Modules:
  0.0 475.3 jit_solution(4424673960620839761)
XLA Ops:
  7.4 69.9 %multiply_convert_fusion.1 = (bf16[4096,1024]{1,0:T(8,128)(2,1)}, bf16[4096,1024]{1,0:T(8,128)(2,1)}) fusion(s32[1024]{0:T(1024)S(1)} %iota_add_fusion.1, f32[4096]{0:T(1024)S(1)} %get-tuple-element.54, f32[4096]{0:T(1024)S(1)} %get-tuple-element.55), kind=kLoop, calls=%fused_computation.31 | loop fusion | flops 75497472 | bytes 16814080 | tf_op jit(solution)/shard_map/convert
  77.4 9.8 %fusion.11 = f32[2048,256]{0,1:T(8,128)} fusion(bf16[256,4096]{1,0:T(8,128)(2,1)S(1)} %bitcast.29, bf16[4096,1024]{1,0:T(8,128)(2,1)} %get-tuple-element.53, bf16[4096,1024]{1,0:T(8,128)(2,1)} %get-tuple-element.52), kind=kOutput, calls=%fused_computation.25 | convolution fusion | flops 4328521728 | bytes 20971520 | tf_op jit(solution)/shard_map/dot_general | solution.py:63
  87.2 1.9 copy.11
  89.5 1.2 fusion.23
  91.0 127.6 %all-gather.2.cloned.1.call-done = bf16[2,1024,2048]{1,2,0:T(8,128)(2,1)} async-done(((bf16[2,128,2048]{1,2,0:T(8,128)(2,1)}), bf16[2,1024,2048]{1,2,0:T(8,128)(2,1)}) %all-gather.2.cloned.1.call-update) | async-done | bytes 8388624 | tf_op jit(solution)/shard_map/all_gather | solution.py:66
  218.5 11.7 %copy.12 = bf16[2,1024,2048]{2,1,0:T(8,128)(2,1)} copy(bf16[2,1024,2048]{1,2,0:T(8,128)(2,1)} %all-gather.2.cloned.1.call-done) | data formatting | bytes 16777216 | tf_op jit(solution)/shard_map/while | solution.py:68
  230.2 32.5 %while.10 = (s32[]{:T(128)}, f32[6,128,2048]{2,1,0:T(8,128)}, s32[6,2]{0,1:T(2,128)S(1)}, bf16[2,1024,2048]{2,1,0:T(8,128)(2,1)}, s32[]{:T(128)}, /*index=5*/s32[1,1]{0,1:T(1,128)}, s32[]{:T(128)}, s32[]{:T(128)}) while((s32[]{:T(128)}, f32[6,128,2048]{2,1,0:T(8,128)}, s32[6,2]{0,1:T(2,128)S(1)}, bf16[2,1024,2048]{2,1,0:T(8,128)(2,1)}, ...), condition=%wide.region_5.6_spmd, body=%wide.region_2.0_spmd.sunk | while | flops 3145738 | bytes 13631721 | solution.py:68
  232.1 1.9 dynamic-slice_convert_fusion.3
  234.6 1.1 fusion.42
  237.5 1.9 dynamic-slice_convert_fusion.3
  240.0 1.1 fusion.42
  242.9 1.9 dynamic-slice_convert_fusion.3
  245.4 1.1 fusion.42
  248.4 1.9 dynamic-slice_convert_fusion.3
  253.8 1.9 dynamic-slice_convert_fusion.3
  256.2 1.1 fusion.42
  259.2 1.9 dynamic-slice_convert_fusion.3
  261.6 1.1 fusion.42
  262.7 9.8 %copy.13 = f32[1,6,128,2048]{3,1,2,0:T(8,128)} copy(f32[1,6,128,2048]{3,2,1,0:T(8,128)} %bitcast.31) | data formatting | bytes 12582912
  272.7 68.4 %fusion.18 = (f32[1024,4096]{1,0:T(8,128)}, f32[1024,4096]{1,0:T(8,128)}) fusion(s32[4096]{0:T(1024)S(1)} %iota_add_fusion, s32[1024]{0:T(1024)S(1)} %iota_add_fusion.1), kind=kLoop, calls=%fused_computation.35 | loop fusion | flops 62914560 | bytes 33574912 | tf_op jit(solution)/shard_map/cos | solution.py:32
  341.2 82.5 %all-reduce.2.cloned.1.call-done = f32[6,262144]{1,0:T(8,128)} async-done(((f32[6,262144]{1,0:T(8,128)}), f32[6,262144]{1,0:T(8,128)}) %all-reduce.2.cloned.1.call-update) | async-done | bytes 6291472 | tf_op jit(solution)/shard_map/psum | solution.py:78
  423.7 7.4 %fusion.27 = f32[2,262144]{1,0:T(2,128)S(1)} fusion(f32[6,262144]{1,0:T(8,128)} %all-reduce.2.cloned.1.call-done, pred[6]{0:T(512)(128)(4,1)S(1)} %compare_bitcast_fusion, s32[6]{0:T(128)S(1)} %convert_reduce_fusion), kind=kOutput, calls=%fused_computation.52 | convolution fusion | flops 37748760 | bytes 8388638 | tf_op jit(solution)/shard_map/dot_general | solution.py:83
  431.1 3.1 reshape.62
  434.2 34.3 %fusion.19 = f32[256,4096]{1,0:T(8,128)} fusion(f32[256,2048]{1,0:T(8,128)} %reshape.62, f32[1024,4096]{1,0:T(8,128)} %get-tuple-element.51, f32[1024,4096]{1,0:T(8,128)} %get-tuple-element.50), kind=kOutput, calls=%fused_computation.36 | convolution fusion | flops 25779240960 | bytes 39845888 | tf_op jit(solution)/shard_map/dot_general | solution.py:87
  (41 shorter events, 9.7 us)
Async XLA Ops:
  6.5 70.9 %copy-start = (bf16[2,128,4096]{2,1,0:T(8,128)(2,1)S(1)}, bf16[2,128,4096]{2,1,0:T(8,128)(2,1)}, u32[]{:S(2)}) copy-start(bf16[2,128,4096]{2,1,0:T(8,128)(2,1)} %param.6) | copy-start | bytes 6291460
  6.5 212.0 %all-gather.2.cloned.1.call-start = ((), (), s32[]{:S(2)}) async-start(), calls=%async_computation | async-start | bytes 9437184 | tf_op jit(solution)/shard_map/all_gather | solution.py:66
  90.7 333.0 %all-reduce.2.cloned.1.call-start = ((), (), s32[]{:S(2)}) async-start(), calls=%async_computation.1 | async-start | bytes 16777216 | tf_op jit(solution)/shard_map/psum | solution.py:78
  91.0 139.3 %copy-start.2 = (s32[1,6,2]{1,2,0:T(2,128)S(1)}, s32[1,6,2]{1,2,0:T(2,128)}, u32[]{:S(2)}) copy-start(s32[1,6,2]{1,2,0:T(2,128)} %param.8) | copy-start | bytes 148
  262.7 9.8 %copy-start.3 = (s32[1,6]{1,0:T(1,128)S(1)}, s32[1,6]{1,0:T(1,128)}, u32[]{:S(2)}) copy-start(s32[1,6]{1,0:T(1,128)} %param.9) | copy-start | bytes 76
  434.2 34.3 %copy-start.1 = (bf16[2,128,4096]{2,1,0:T(8,128)(2,1)S(1)}, bf16[2,128,4096]{2,1,0:T(8,128)(2,1)}, u32[]{:S(2)}) copy-start(bf16[2,128,4096]{2,1,0:T(8,128)(2,1)} %param.6) | copy-start | bytes 6291460
Sparse Core Ops, SparseCore 0:
  90.9 127.6 all-gather.1
  272.6 151.0 all-reduce.1
where the time goes:
time: 476 us; the launch traced here: 475 us
  waiting for transfers between devices  210 us (44%)
  other arithmetic  162 us (34%)
  matrix products  51.5 us (11%)
  local copies, waits for them, and re-layouts  30.2 us (6%)
  between operations  13.5 us (3%)
  loops' own time  7.78 us (2%)
    all_gather x1, waiting for transfers between devices, local(): gathered = lax.all_gather(white, 'ch', axis=1, tiled=True)  128 us
    psum x1, waiting for transfers between devices, local(): summed = lax.psum(flat_partial, 'grp')  82.5 us
    another operation x1, other arithmetic  69.9 us
    cos x1, other arithmetic, inverse_table(): return jnp.concatenate([jnp.cos(angles), -jnp.sin(angles)], axis=0)  68.4 us
    dot_general x1, matrix products, local(): jnp.dot(total.reshape(-1, 2 * NB), inverse, precision=lax.Precision.HIGHE...  34.3 us
    while x1, local copies, waits for them, and re-layouts, local(): lax.map(lambda pair_entry: cross_block(gathered, pair_entry, BLK, NB), pa...  11.7 us
    convert_element_type x6, other arithmetic, cross_block(): lax.dynamic_slice_in_dim(rows, pair_entry[0] * block, block, 1)  11.3 us
    dot_general x1, matrix products, local(): jnp.dot(strain.reshape(-1, NFFT), forward, preferred_element_type=jnp.flo...  9.8 us
  transfers between devices with their start and end apart: 2, of which 2 were waited for; matrix products, arithmetic and copies ran while one was open for 14% of the time, Pallas kernels for 0%

commit v1 on v0

--- a/solution.py
+++ b/solution.py
@@ -9,6 +9,20 @@
 SUB = 64
 BLK = 128
 CAP = 2
+
+
+def group_lines(s0):
+    how_many = lax.axis_size("ch")
+    tray = []
+    for c in tuple(range(how_many)):
+        tray.append((c, (c + 1) % how_many))
+    current_block = [None] * how_many
+    current_block[how_many - 1] = s0
+    for dd in range(how_many - 2, -1, -1):
+        current_block[dd] = lax.ppermute(current_block[dd + 1], axis_name="ch", perm=tray)
+    wide_out = jnp.concatenate(current_block, axis=1)
+    base_arr = lax.axis_index("ch")
+    return jnp.roll(wide_out, shift=(base_arr + 1) * s0.shape[1], axis=1)
 
 
 def forward_table(length, bins):
@@ -63,7 +77,7 @@
     spectrum = jnp.dot(strain.reshape(-1, NFFT), forward, preferred_element_type=jnp.float32)
     spectrum = spectrum.reshape(strain.shape[0], strain.shape[1], 2 * NB)
     white = whiten_rows(spectrum, valid_mask, NB, SUB)
-    gathered = lax.all_gather(white, "ch", axis=1, tiled=True)
+    gathered = group_lines(white)
     pair_codes = pair_list[0]
     partial_value = lax.map(
         lambda pair_entry: cross_block(gathered, pair_entry, BLK, NB), pair_codes

time: 476 us -> 563 us (1.18)
  waiting for transfers between devices: 210 us -> 256 us
  local copies, waits for them, and re-layouts: 30.2 us -> 67.6 us
    ppermute x0 -> x7, waiting for transfers between devices: none -> 176 us  [group_lines(): lax.ppermute(current_block[dd + 1], axis_name='ch', perm=tray)]
    all_gather x1 -> x0, waiting for transfers between devices: 128 us -> none  [local(): gathered = lax.all_gather(white, 'ch', axis=1, tiled=True)]
    unnamed x9 -> x38, local copies, waits for them, and re-layouts: 9.79 us -> 38.2 us
    dynamic_slice x0 -> x1, local copies, waits for them, and re-layouts: none -> 7.6 us  [group_lines(): return jnp.roll(wide_out, shift=(base_arr + 1) * s0.shape[1], axis=1)]
  transfers between devices with their start and end apart: 2 -> 8, of which waited for: 2 -> 8; matrix products, arithmetic and copies ran while one was open for 14% -> 12% of each run, Pallas kernels for 0% -> 0%
where the time goes in v1:
time: 563 us; the launch traced here: 562 us
  waiting for transfers between devices  256 us (45%)
  other arithmetic  162 us (29%)
  local copies, waits for them, and re-layouts  67.6 us (12%)
  matrix products  51.5 us (9%)
  between operations  13.5 us (2%)
  loops' own time  7.79 us (1%)
    ppermute x7, waiting for transfers between devices, group_lines(): lax.ppermute(current_block[dd + 1], axis_name='ch', perm=tray)  176 us
    psum x1, waiting for transfers between devices, local(): summed = lax.psum(flat_partial, 'grp')  80.5 us
    another operation x1, other arithmetic  70 us
    cos x1, other arithmetic, inverse_table(): return jnp.concatenate([jnp.cos(angles), -jnp.sin(angles)], axis=0)  68.4 us
    unnamed x38, local copies, waits for them, and re-layouts  38.2 us
    dot_general x1, matrix products, local(): jnp.dot(total.reshape(-1, 2 * NB), inverse, precision=lax.Precision.HIGHE...  34.2 us
    convert_element_type x6, other arithmetic, cross_block(): lax.dynamic_slice_in_dim(rows, pair_entry[0] * block, block, 1)  12.4 us
    while x1, local copies, waits for them, and re-layouts, local(): lax.map(lambda pair_entry: cross_block(gathered, pair_entry, BLK, NB), pa...  11.7 us
  transfers between devices with their start and end apart: 8, of which 8 were waited for; matrix products, arithmetic and copies ran while one was open for 12% of the time, Pallas kernels for 0%

profile of v1, /device:TPU:0, one launch (start us, length us, event | category | flops | bytes accessed | tf_op | source)
XLA Modules:
  0.0 561.6 jit_solution(5710102013157547280)
XLA Ops:
  6.6 70.0 %multiply_convert_fusion.1 = (bf16[4096,1024]{1,0:T(8,128)(2,1)}, bf16[4096,1024]{1,0:T(8,128)(2,1)}) fusion(s32[1024]{0:T(1024)S(1)} %iota_add_fusion.1, f32[4096]{0:T(1024)S(1)} %get-tuple-element.54, f32[4096]{0:T(1024)S(1)} %get-tuple-element.55), kind=kLoop, calls=%fused_computation.31 | loop fusion | flops 75497472 | bytes 16814080 | tf_op jit(solution)/shard_map/convert
  76.7 9.8 %fusion.11 = f32[2048,256]{0,1:T(8,128)} fusion(bf16[256,4096]{1,0:T(8,128)(2,1)S(1)} %bitcast.29, bf16[4096,1024]{1,0:T(8,128)(2,1)} %get-tuple-element.53, bf16[4096,1024]{1,0:T(8,128)(2,1)} %get-tuple-element.52), kind=kOutput, calls=%fused_computation.25 | convolution fusion | flops 4328521728 | bytes 20971520 | tf_op jit(solution)/shard_map/dot_general | solution.py:77
  89.0 3.0 collective-permute-start
  92.1 26.2 %collective-permute-done = bf16[2,128,2048]{1,2,0:T(8,128)(2,1)S(1)} collective-permute-done((bf16[2,128,2048]{1,2,0:T(8,128)(2,1)S(1)}, bf16[2,128,2048]{1,2,0:T(8,128)(2,1)S(1)}, u32[]{:S(2)}, u32[]{:S(2)}) %collective-permute-start) | collective-permute-done | bytes 1048608 | tf_op jit(solution)/shard_map/ppermute | solution.py:22
  118.3 27.0 %collective-permute-done.1 = bf16[2,128,2048]{1,2,0:T(8,128)(2,1)S(1)} collective-permute-done((bf16[2,128,2048]{1,2,0:T(8,128)(2,1)S(1)}, bf16[2,128,2048]{1,2,0:T(8,128)(2,1)S(1)}, u32[]{:S(2)}, u32[]{:S(2)}) %collective-permute-start.1) | collective-permute-done | bytes 1048608 | tf_op jit(solution)/shard_map/ppermute | solution.py:22
  145.3 26.2 %collective-permute-done.2 = bf16[2,128,2048]{1,2,0:T(8,128)(2,1)S(1)} collective-permute-done((bf16[2,128,2048]{1,2,0:T(8,128)(2,1)S(1)}, bf16[2,128,2048]{1,2,0:T(8,128)(2,1)S(1)}, u32[]{:S(2)}, u32[]{:S(2)}) %collective-permute-start.2) | collective-permute-done | bytes 1048608 | tf_op jit(solution)/shard_map/ppermute | solution.py:22
  172.4 25.3 %collective-permute-done.3 = bf16[2,128,2048]{1,2,0:T(8,128)(2,1)S(1)} collective-permute-done((bf16[2,128,2048]{1,2,0:T(8,128)(2,1)S(1)}, bf16[2,128,2048]{1,2,0:T(8,128)(2,1)S(1)}, u32[]{:S(2)}, u32[]{:S(2)}) %collective-permute-start.3) | collective-permute-done | bytes 1048608 | tf_op jit(solution)/shard_map/ppermute | solution.py:22
  198.7 24.4 %collective-permute-done.4 = bf16[2,128,2048]{1,2,0:T(8,128)(2,1)S(1)} collective-permute-done((bf16[2,128,2048]{1,2,0:T(8,128)(2,1)S(1)}, bf16[2,128,2048]{1,2,0:T(8,128)(2,1)S(1)}, u32[]{:S(2)}, u32[]{:S(2)}) %collective-permute-start.4) | collective-permute-done | bytes 1048608 | tf_op jit(solution)/shard_map/ppermute | solution.py:22
  224.2 23.7 %collective-permute-done.5 = bf16[2,128,2048]{1,2,0:T(8,128)(2,1)} collective-permute-done((bf16[2,128,2048]{1,2,0:T(8,128)(2,1)S(1)}, bf16[2,128,2048]{1,2,0:T(8,128)(2,1)}, u32[]{:S(2)}, u32[]{:S(2)}) %collective-permute-start.5) | collective-permute-done | bytes 1048608 | tf_op jit(solution)/shard_map/ppermute | solution.py:22
  247.9 23.0 %collective-permute-done.6 = bf16[2,128,2048]{1,2,0:T(8,128)(2,1)} collective-permute-done((bf16[2,128,2048]{1,2,0:T(8,128)(2,1)}, bf16[2,128,2048]{1,2,0:T(8,128)(2,1)}, u32[]{:S(2)}, u32[]{:S(2)}) %collective-permute-start.6) | collective-permute-done | bytes 1048608 | tf_op jit(solution)/shard_map/ppermute | solution.py:22
  270.9 2.3 constant_dynamic-update-slice_fusion.15
  273.3 2.4 constant_dynamic-update-slice_fusion.14
  275.6 2.4 constant_dynamic-update-slice_fusion.13
  280.3 2.4 constant_dynamic-update-slice_fusion.11
  288.4 2.4 constant_dynamic-update-slice_fusion.6
  297.5 7.6 %constant_dynamic-slice_fusion.1 = bf16[2,1024,2048]{1,2,0:T(8,128)(2,1)} fusion(bf16[2,2048,2048]{1,2,0:T(8,128)(2,1)} %constant_dynamic-update-slice_fusion, s32[]{:T(128)S(6)} %select_n.37), kind=kLoop, calls=%fused_computation.75 | loop fusion | bytes 16777220 | tf_op jit(solution)/shard_map/jit(_roll_dynamic)/dynamic_slice | solution.py:25
  305.1 11.7 %copy.12 = bf16[2,1024,2048]{2,1,0:T(8,128)(2,1)} copy(bf16[2,1024,2048]{1,2,0:T(8,128)(2,1)} %constant_dynamic-slice_fusion.1) | data formatting | bytes 16777216 | tf_op jit(solution)/shard_map/while | solution.py:82
  316.7 34.2 %while.10 = (s32[]{:T(128)}, f32[6,128,2048]{2,1,0:T(8,128)}, s32[6,2]{0,1:T(2,128)S(1)}, bf16[2,1024,2048]{2,1,0:T(8,128)(2,1)}, s32[]{:T(128)}, /*index=5*/s32[1,1]{0,1:T(1,128)}, s32[]{:T(128)}, s32[]{:T(128)}) while((s32[]{:T(128)}, f32[6,128,2048]{2,1,0:T(8,128)}, s32[6,2]{0,1:T(2,128)S(1)}, bf16[2,1024,2048]{2,1,0:T(8,128)(2,1)}, ...), condition=%wide.region_5.6_spmd, body=%wide.region_2.5_spmd.sunk | while | flops 3145738 | bytes 13632221 | solution.py:82
  351.0 9.8 %copy.13 = f32[1,6,128,2048]{3,1,2,0:T(8,128)} copy(f32[1,6,128,2048]{3,2,1,0:T(8,128)} %bitcast.31) | data formatting | bytes 12582912
  361.0 68.4 %fusion.18 = (f32[1024,4096]{1,0:T(8,128)}, f32[1024,4096]{1,0:T(8,128)}) fusion(s32[4096]{0:T(1024)S(1)} %iota_add_fusion, s32[1024]{0:T(1024)S(1)} %iota_add_fusion.1), kind=kLoop, calls=%fused_computation.35 | loop fusion | flops 62914560 | bytes 33574912 | tf_op jit(solution)/shard_map/cos | solution.py:46
  429.4 80.5 %all-reduce.2.cloned.1.call-done = f32[6,262144]{1,0:T(8,128)} async-done(((f32[6,262144]{1,0:T(8,128)}), f32[6,262144]{1,0:T(8,128)}) %all-reduce.2.cloned.1.call-update) | async-done | bytes 6291472 | tf_op jit(solution)/shard_map/psum | solution.py:92
  509.9 7.4 %fusion.27 = f32[2,262144]{1,0:T(2,128)S(1)} fusion(f32[6,262144]{1,0:T(8,128)} %all-reduce.2.cloned.1.call-done, pred[6]{0:T(512)(128)(4,1)S(1)} %compare_bitcast_fusion, s32[6]{0:T(128)S(1)} %convert_reduce_fusion), kind=kOutput, calls=%fused_computation.68 | convolution fusion | flops 37748760 | bytes 8388638 | tf_op jit(solution)/shard_map/dot_general | solution.py:97
  517.3 3.1 reshape.62
  520.5 34.2 %fusion.19 = f32[256,4096]{1,0:T(8,128)} fusion(f32[256,2048]{1,0:T(8,128)} %reshape.62, f32[1024,4096]{1,0:T(8,128)} %get-tuple-element.51, f32[1024,4096]{1,0:T(8,128)} %get-tuple-element.50), kind=kOutput, calls=%fused_computation.36 | convolution fusion | flops 25779240960 | bytes 39845888 | tf_op jit(solution)/shard_map/dot_general | solution.py:101
  (83 shorter events, 46.9 us)
Async XLA Ops:
  6.5 70.1 %copy-start = (bf16[2,128,4096]{2,1,0:T(8,128)(2,1)S(1)}, bf16[2,128,4096]{2,1,0:T(8,128)(2,1)}, u32[]{:S(2)}) copy-start(bf16[2,128,4096]{2,1,0:T(8,128)(2,1)} %param.6) | copy-start | bytes 6291460
  6.5 503.4 %all-reduce.2.cloned.1.call-start = ((), (), s32[]{:S(2)}) async-start(), calls=%async_computation | async-start | bytes 16777216 | tf_op jit(solution)/shard_map/psum | solution.py:92
  76.7 12.0 %copy-start.9 = (s32[2,128]{1,0:T(2,128)S(1)}, s32[2,128]{1,0:T(2,128)}, u32[]{:S(2)}) copy-start(s32[2,128]{1,0:T(2,128)} %param.7) | copy-start | bytes 3076
  89.0 29.2 %collective-permute-start = (bf16[2,128,2048]{1,2,0:T(8,128)(2,1)S(1)}, bf16[2,128,2048]{1,2,0:T(8,128)(2,1)S(1)}, u32[]{:S(2)}, u32[]{:S(2)}) collective-permute-start(bf16[2,128,2048]{1,2,0:T(8,128)(2,1)S(1)} %fusion.23), channel_id=1, source_target_pairs={{0,1},{1,2},{2,3},{3,4},{4,5},{5,6},{6,7},{7,0},{8,9},{9,10},{10,1... | collective-permute-start | bytes 3145736 | tf_op jit(solution)/shard_map/ppermute | solution.py:22
  118.3 27.0 %collective-permute-start.1 = (bf16[2,128,2048]{1,2,0:T(8,128)(2,1)S(1)}, bf16[2,128,2048]{1,2,0:T(8,128)(2,1)S(1)}, u32[]{:S(2)}, u32[]{:S(2)}) collective-permute-start(bf16[2,128,2048]{1,2,0:T(8,128)(2,1)S(1)} %collective-permute-done), channel_id=1, source_target_pairs={{0,1},{1,2},{2,3},{3,4},{4,5},{5,6},{6,7},{7,0},{8,9},{9,10},{10,1... | collective-permute-start | bytes 3145736 | tf_op jit(solution)/shard_map/ppermute | solution.py:22
  145.3 26.2 %collective-permute-start.2 = (bf16[2,128,2048]{1,2,0:T(8,128)(2,1)S(1)}, bf16[2,128,2048]{1,2,0:T(8,128)(2,1)S(1)}, u32[]{:S(2)}, u32[]{:S(2)}) collective-permute-start(bf16[2,128,2048]{1,2,0:T(8,128)(2,1)S(1)} %collective-permute-done.1), channel_id=1, source_target_pairs={{0,1},{1,2},{2,3},{3,4},{4,5},{5,6},{6,7},{7,0},{8,9},{9,10},{10,1... | collective-permute-start | bytes 3145736 | tf_op jit(solution)/shard_map/ppermute | solution.py:22
  171.4 1.0 copy-start.2
  172.4 25.3 %collective-permute-start.3 = (bf16[2,128,2048]{1,2,0:T(8,128)(2,1)S(1)}, bf16[2,128,2048]{1,2,0:T(8,128)(2,1)S(1)}, u32[]{:S(2)}, u32[]{:S(2)}) collective-permute-start(bf16[2,128,2048]{1,2,0:T(8,128)(2,1)S(1)} %collective-permute-done.2), channel_id=1, source_target_pairs={{0,1},{1,2},{2,3},{3,4},{4,5},{5,6},{6,7},{7,0},{8,9},{9,10},{10,1... | collective-permute-start | bytes 3145736 | tf_op jit(solution)/shard_map/ppermute | solution.py:22
  197.7 1.0 copy-start.4
  198.7 24.5 %collective-permute-start.4 = (bf16[2,128,2048]{1,2,0:T(8,128)(2,1)S(1)}, bf16[2,128,2048]{1,2,0:T(8,128)(2,1)S(1)}, u32[]{:S(2)}, u32[]{:S(2)}) collective-permute-start(bf16[2,128,2048]{1,2,0:T(8,128)(2,1)S(1)} %collective-permute-done.3), channel_id=1, source_target_pairs={{0,1},{1,2},{2,3},{3,4},{4,5},{5,6},{6,7},{7,0},{8,9},{9,10},{10,1... | collective-permute-start | bytes 3145736 | tf_op jit(solution)/shard_map/ppermute | solution.py:22
  223.2 1.0 copy-start.6
  224.2 23.7 %collective-permute-start.5 = (bf16[2,128,2048]{1,2,0:T(8,128)(2,1)S(1)}, bf16[2,128,2048]{1,2,0:T(8,128)(2,1)}, u32[]{:S(2)}, u32[]{:S(2)}) collective-permute-start(bf16[2,128,2048]{1,2,0:T(8,128)(2,1)S(1)} %collective-permute-done.4), channel_id=1, source_target_pairs={{0,1},{1,2},{2,3},{3,4},{4,5},{5,6},{6,7},{7,0},{8,9},{9,10},{10,1... | collective-permute-start | bytes 3145736 | tf_op jit(solution)/shard_map/ppermute | solution.py:22
  247.9 23.1 %collective-permute-start.6 = (bf16[2,128,2048]{1,2,0:T(8,128)(2,1)}, bf16[2,128,2048]{1,2,0:T(8,128)(2,1)}, u32[]{:S(2)}, u32[]{:S(2)}) collective-permute-start(bf16[2,128,2048]{1,2,0:T(8,128)(2,1)} %collective-permute-done.5), channel_id=1, source_target_pairs={{0,1},{1,2},{2,3},{3,4},{4,5},{5,6},{6,7},{7,0},{8,9},{9,10},{10,1... | collective-permute-start | bytes 3145736 | tf_op jit(solution)/shard_map/ppermute | solution.py:22
  247.9 42.9 %copy-start.7 = (bf16[2,128,2048]{1,2,0:T(8,128)(2,1)S(1)}, bf16[2,128,2048]{1,2,0:T(8,128)(2,1)}, u32[]{:S(2)}) copy-start(bf16[2,128,2048]{1,2,0:T(8,128)(2,1)} %copy-done.6) | copy-start | bytes 3145732
  247.9 44.1 %copy-start.5 = (bf16[2,128,2048]{1,2,0:T(8,128)(2,1)S(1)}, bf16[2,128,2048]{1,2,0:T(8,128)(2,1)}, u32[]{:S(2)}) copy-start(bf16[2,128,2048]{1,2,0:T(8,128)(2,1)} %copy-done.4) | copy-start | bytes 3145732
  247.9 45.2 %copy-start.3 = (bf16[2,128,2048]{1,2,0:T(8,128)(2,1)S(1)}, bf16[2,128,2048]{1,2,0:T(8,128)(2,1)}, u32[]{:S(2)}) copy-start(bf16[2,128,2048]{1,2,0:T(8,128)(2,1)} %copy-done.2) | copy-start | bytes 3145732
  297.5 19.3 %copy-start.8 = (s32[1,6,2]{1,2,0:T(2,128)S(1)}, s32[1,6,2]{1,2,0:T(2,128)}, u32[]{:S(2)}) copy-start(s32[1,6,2]{1,2,0:T(2,128)} %param.8) | copy-start | bytes 148
  351.0 9.8 %copy-start.10 = (s32[1,6]{1,0:T(1,128)S(1)}, s32[1,6]{1,0:T(1,128)}, u32[]{:S(2)}) copy-start(s32[1,6]{1,0:T(1,128)} %param.9) | copy-start | bytes 76
  520.5 34.3 %copy-start.1 = (bf16[2,128,4096]{2,1,0:T(8,128)(2,1)S(1)}, bf16[2,128,4096]{2,1,0:T(8,128)(2,1)}, u32[]{:S(2)}) copy-start(bf16[2,128,4096]{2,1,0:T(8,128)(2,1)} %param.6) | copy-start | bytes 6291460
Sparse Core Ops, SparseCore 0:
  360.9 148.9 all-reduce.1
